TPU v7x, 32 devices: a whole 2x2x4 slice. The times are simulated.
32 devices in a mesh: shot: 16 (over z, y, core), rcv: 2 (over x).
Axes of the slice: x: 2, y: 2, z: 4, core: 2. Of those that a mesh axis runs over, the one named last changes fastest.
Arguments:
- record: bfloat16 [768, 131072], P('rcv', 'shot'), may hold values from -6 to 6
- shot_fire_samples: int32 [512], P('shot'), may hold values from 0 to 131071, as said below
Outputs:
- psf_gram: float32 [2, 4, 768, 768], P(None, None, 'rcv', 'shot')
Inputs may be any that keep to these rules, and one draw needn't show every extreme that they name: `shot_fire_samples`: shot s fires at a sample from s * 256 to s * 256 + 255.
All inputs are finite; a program needn't handle non-finite values.
Results may differ from a plain program's by a relative error of at most 0.0025.
Values may be sent and summed in bfloat16 or wider, within the bound.
A program may use at most 64 MiB of HBM per device.

v0:
```python
import math

import jax
import jax.numpy as jnp
from jax import lax
from jax.sharding import PartitionSpec as P

WIN = 2048
SPACING = 256


freq_bins = (24, 40, 56, 80)


def shifted(block, axis, distance):
    devices = range(lax.axis_size(axis))
    route = [(i - distance, i) for i in devices if i - distance in devices]
    return lax.ppermute(block, axis, route)


def dft_table(window_len):
    lag_index = jnp.arange(window_len, dtype=jnp.int32)
    bin_list = jnp.array(freq_bins, dtype=jnp.int32)
    turn_count = lag_index[:, None] * bin_list[None, :] % window_len
    phase_angle = 2.0 * math.pi / window_len * turn_count.astype(jnp.float32)
    dft_rows = jnp.concatenate([jnp.cos(phase_angle), -jnp.sin(phase_angle)], axis=1) / math.sqrt(
        window_len
    )
    return dft_rows.astype(jnp.bfloat16)


def shifted_tables(jitter, span):
    lag_index = jnp.arange(span, dtype=jnp.int32)[None, :] - jitter[:, None]
    inside = (lag_index >= 0) & (lag_index < WIN)
    clipped = jnp.clip(lag_index, 0, WIN - 1)
    bin_list = jnp.array(freq_bins, dtype=jnp.int32)
    turn_count = clipped[:, None, :] * bin_list[None, :, None] % WIN
    phase_angle = 2.0 * math.pi / WIN * turn_count.astype(jnp.float32)
    table = jnp.concatenate([jnp.cos(phase_angle), -jnp.sin(phase_angle)], axis=1) / math.sqrt(WIN)
    table = jnp.where(inside[:, None, :], table, 0.0)
    return table.astype(jnp.bfloat16)


def local_spectra(extended, sample_offsets, dft_rows):
    count_of_shots = sample_offsets.shape[0]
    reach_blocks = WIN // SPACING + 1
    jitter = sample_offsets - jnp.arange(count_of_shots, dtype=jnp.int32) * SPACING
    tables = shifted_tables(jitter, reach_blocks * SPACING)
    tables = tables.reshape(count_of_shots, dft_rows.shape[1], reach_blocks, SPACING)
    blocks = extended.reshape(extended.shape[0], extended.shape[1] // SPACING, SPACING)
    total = jnp.zeros((count_of_shots, dft_rows.shape[1], extended.shape[0]), jnp.float32)
    for offset in range(reach_blocks):
        record_part = blocks[:, offset : offset + count_of_shots, :]
        total = total + jnp.einsum(
            "rsu,scu->scr", record_part, tables[:, :, offset, :], preferred_element_type=jnp.float32
        )
    return total


def gram_terms(left, right):
    nfreq = len(freq_bins)
    left_re = left[:, :nfreq, :]
    left_im = left[:, nfreq:, :]
    right_re = right[:, :nfreq, :]
    right_im = right[:, nfreq:, :]
    gram_real = jnp.einsum("sfr,sfq->frq", left_re, right_re, preferred_element_type=jnp.float32)
    gram_real = gram_real + jnp.einsum(
        "sfr,sfq->frq", left_im, right_im, preferred_element_type=jnp.float32
    )
    gram_imag = jnp.einsum("sfr,sfq->frq", left_re, right_im, preferred_element_type=jnp.float32)
    gram_imag = gram_imag - jnp.einsum(
        "sfr,sfq->frq", left_im, right_re, preferred_element_type=jnp.float32
    )
    return jnp.stack([gram_real, gram_imag], axis=0)


def per_device(record, shot_fire_samples):
    trace_segment_length = record.shape[1]
    count_of_shots = shot_fire_samples.shape[0]
    dft_rows = dft_table(WIN)
    sample_offsets = shot_fire_samples - lax.axis_index("shot") * trace_segment_length
    head_rows = record[:, :WIN]
    rim_rows = shifted(head_rows, "shot", -1)
    extended = jnp.concatenate([record, rim_rows], axis=1)
    trace_spectra = local_spectra(extended, sample_offsets, dft_rows)
    trace_spectra = trace_spectra.astype(jnp.bfloat16)
    all_receivers = lax.all_gather(trace_spectra, "rcv", axis=2, tiled=True)
    total_shots = count_of_shots * lax.axis_size("shot")
    row_side = lax.all_gather(trace_spectra, "shot", axis=0, tiled=True)
    column_side = lax.all_to_all(all_receivers, "shot", split_axis=2, concat_axis=0, tiled=True)
    result = gram_terms(row_side, column_side)
    return result / total_shots


def solution(mesh):
    return jax.shard_map(
        per_device,
        mesh=mesh,
        in_specs=(P("rcv", "shot"), P("shot")),
        out_specs=P(None, None, "rcv", "shot"),
        check_vma=False,
    )
```

profile of v0, /device:TPU:0, one launch (start us, length us, event | category | flops | bytes accessed | tf_op | source)
XLA Modules:
  0.0 125.5 jit_solution(16879435166929564003)
XLA Ops:
  6.5 8.6 %copy.41 = bf16[384,8192]{0,1:T(8,128)(2,1)} copy(bf16[384,8192]{1,0:T(8,128)(2,1)} %param.3) | data formatting | bytes 12582912 | tf_op args[0]
  15.2 1.6 %slice.93 = bf16[384,2048]{0,1:T(8,128)(2,1)S(1)} slice(bf16[384,8192]{0,1:T(8,128)(2,1)} %copy.41), slice={[0:384], [0:2048]} | slice | bytes 3145728 | tf_op jit(solution)/shard_map/slice | solution.py:82
  16.8 1.3 %collective-permute-start = (bf16[384,2048]{0,1:T(8,128)(2,1)S(1)}, bf16[384,2048]{0,1:T(8,128)(2,1)S(1)}, u32[]{:S(2)}, u32[]{:S(2)}) collective-permute-start(bf16[384,2048]{0,1:T(8,128)(2,1)S(1)} %slice.93), channel_id=1, source_target_pairs={{2,0},{4,2},{6,4},{8,6},{10,8},{12,10},{14,12},{16,14},{18,16},{20... | collective-permute-start | bytes 4718600 | tf_op jit(solution)/shard_map/ppermute | solution.py:18
  18.4 9.7 %fusion.70 = (f32[32,4,9,256]{3,1,0,2:T(4,128)S(1)}, f32[32,4,9,256]{3,1,0,2:T(4,128)S(1)}) fusion(s32[4]{0:T(128)S(1)} %copy-done.1, s32[32,9,256]{2,0,1:T(8,128)S(1)} %subtract_clamp_fusion), kind=kLoop, calls=%fused_computation.54 | loop fusion | flops 4423680 | bytes 2654224 | tf_op jit(solution)/shard_map/cos | solution.py:39
  28.1 0.8 fusion.19
  29.0 14.8 %pad_maximum_fusion = bf16[384,10240]{0,1:T(8,128)(2,1)S(1)} fusion(bf16[384,2048]{0,1:T(8,128)(2,1)S(1)} %collective-permute-done, bf16[384,8192]{0,1:T(8,128)(2,1)S(1)} %copy-done), kind=kLoop, calls=%fused_computation | loop fusion | flops 15728640 | bytes 15728640 | tf_op jit(solution)/shard_map/concatenate | solution.py:84
  43.9 0.9 fusion
  44.8 0.9 fusion.2
  45.7 0.9 fusion.4
  46.6 0.9 fusion.6
  47.6 0.9 fusion.8
  48.5 0.9 fusion.10
  49.4 0.9 fusion.12
  50.4 0.9 fusion.14
  51.3 1.6 %fusion.55 = bf16[32,8,384]{2,1,0:T(8,128)(2,1)} fusion(f32[32,8,384]{2,1,0:T(8,128)S(1)} %fusion, f32[32,8,384]{2,1,0:T(8,128)S(1)} %fusion.2, f32[32,8,384]{2,1,0:T(8,128)S(1)} %fusion.4, f32[32,8,384]{2,1,0:T(8,128)S(1)} %fusion.6, f32[32,8,384]{2,1,0:T(8,128)S(1)} %fusion.8, f32[32,8,384]{2,1,0:T(8,128)S(1)} %fusion.10, f32[32,8,384]{2,1,0:T(8,128)S(1)} %fusion.12, ...), kind=kOutput, calls=%fused_computation.48 | convolution fusion | flops 51216384 | bytes 9764864 | tf_op jit(solution)/shard_map/rsu,scu->scr/dot_general | solution.py:54
  52.9 7.5 %all_gather.7 = bf16[32,8,768]{2,1,0:T(8,128)(2,1)S(1)} all-gather(bf16[32,8,384]{2,1,0:T(8,128)(2,1)} %fusion.55), channel_id=1, replica_groups=mesh['shot'=16,'rcv'=2] {'rcv'}, dimensions={2}, use_global_device_ids=true | all-gather | bytes 589824 | tf_op jit(solution)/shard_map/all_gather | solution.py:87
  60.5 1.2 copy.52
  61.6 1.5 %reshape.59 = bf16[16,2,6144]{2,1,0:T(2,128)(2,1)S(1)} reshape(bf16[768,8,32]{2,1,0:T(8,128)(2,1)S(1)} %bitcast.53) | data formatting | bytes 786432
  63.1 28.9 %all_to_all.18 = bf16[16,2,6144]{2,1,0:T(2,128)(2,1)S(1)} all-to-all(bf16[16,2,6144]{2,1,0:T(2,128)(2,1)S(1)} %reshape.59), channel_id=1, replica_groups=mesh['shot'=16,'rcv'=2] {'shot'}, dimensions={0} | all-to-all | bytes 786432 | tf_op jit(solution)/shard_map/all_to_all | solution.py:90
  92.8 1.0 copy.83
  93.8 1.5 %all_to_all.16 = bf16[512,8,48]{0,2,1:T(8,128)(2,1)S(1)} reshape(bf16[16,32,8,48]{1,0,3,2:T(8,128)(2,1)S(1)} %bitcast.52) | data formatting | bytes 786432 | tf_op jit(solution)/shard_map/all_to_all | solution.py:90
  95.3 16.9 %all-gather.2.cloned.1.call-done = bf16[512,8,384]{2,1,0:T(8,128)(2,1)} async-done(((bf16[32,8,384]{2,1,0:T(8,128)(2,1)}), bf16[512,8,384]{2,1,0:T(8,128)(2,1)}) %all-gather.2.cloned.1.call-update) | async-done | bytes 3145744 | tf_op jit(solution)/shard_map/all_gather | solution.py:89
  112.3 4.1 %fusion.76 = (bf16[512,4,384]{2,1,0:T(4,128)(2,1)S(1)}, bf16[512,4,384]{2,1,0:T(4,128)(2,1)S(1)}) fusion(bf16[512,8,384]{2,1,0:T(8,128)(2,1)} %all-gather.2.cloned.1.call-done), kind=kLoop, calls=%fused_computation.74 | loop fusion | bytes 6291456 | tf_op jit(solution)/shard_map/slice | solution.py:62
  117.8 0.9 maximum_multiply_fusion.1
  (18 shorter events, 2.5 us)
Async XLA Ops:
  6.5 105.7 %all-gather.2.cloned.1.call-start = ((), (), s32[]{:S(2)}) async-start(), calls=%async_computation.1 | async-start | bytes 3342336 | tf_op jit(solution)/shard_map/all_gather | solution.py:89
  15.2 2.9 %copy-start.2 = (s32[32]{0:T(128)S(1)}, s32[32]{0:T(128)}, u32[]{:S(2)}) copy-start(s32[32]{0:T(128)} %param.4) | copy-start | bytes 388
  15.2 3.2 %copy-start.1 = (s32[4]{0:T(128)S(1)}, s32[4]{0:T(128)}, u32[]{:S(2)}) copy-start(s32[4]{0:T(128)} %constant.43.clone) | copy-start | bytes 52
  16.8 12.2 %collective-permute-start = (bf16[384,2048]{0,1:T(8,128)(2,1)S(1)}, bf16[384,2048]{0,1:T(8,128)(2,1)S(1)}, u32[]{:S(2)}, u32[]{:S(2)}) collective-permute-start(bf16[384,2048]{0,1:T(8,128)(2,1)S(1)} %slice.93), channel_id=1, source_target_pairs={{2,0},{4,2},{6,4},{8,6},{10,8},{12,10},{14,12},{16,14},{18,16},{20... | collective-permute-start | bytes 4718600 | tf_op jit(solution)/shard_map/ppermute | solution.py:18
  18.3 10.8 %copy-start = (bf16[384,8192]{0,1:T(8,128)(2,1)S(1)}, bf16[384,8192]{0,1:T(8,128)(2,1)}, u32[]{:S(2)}) copy-start(bf16[384,8192]{0,1:T(8,128)(2,1)} %copy.41) | copy-start | bytes 18874372
Sparse Core Ops, SparseCore 0:
  53.0 59.1 all-gather.1
where the time goes:
time: 126 us
  blocking collectives  36.5 us (29%)
  other arithmetic  26.6 us (21%)
  local copies, waits for them, and re-layouts  20.2 us (16%)
  waiting for transfers between devices  17 us (13%)
  between operations  13.6 us (11%)
  matrix products  10.5 us (8%)
  starting transfers between devices  1.29 us (1%)
    all_to_all x1, blocking collectives, per_device(): lax.all_to_all(all_receivers, 'shot', split_axis=2, concat_axis=0, tiled=...  28.9 us
    all_gather x1, waiting for transfers between devices, per_device(): row_side = lax.all_gather(trace_spectra, 'shot', axis=0, tiled=True)  16.9 us
    concatenate x1, other arithmetic, per_device(): extended = jnp.concatenate([record, rim_rows], axis=1)  14.8 us
    unnamed x9, local copies, waits for them, and re-layouts  10.9 us
    cos x1, other arithmetic, shifted_tables(): jnp.cos(phase_angle)  9.74 us
    dot_general x9, matrix products, local_spectra(): jnp.einsum('rsu,scu->scr', record_part, tables[:, :, offset, :], preferre...  9.03 us
    all_gather x1, blocking collectives, per_device(): all_receivers = lax.all_gather(trace_spectra, 'rcv', axis=2, tiled=True)  7.55 us
    slice x1, local copies, waits for them, and re-layouts, gram_terms(): left_re = left[:, :nfreq, :]  4.06 us
  transfers between devices with their start and end apart: 2, of which 1 were waited for; matrix products, arithmetic and copies ran while one was open for 12% of the time, Pallas kernels for 0%

commit v1 on v0

--- a/solution.py
+++ b/solution.py
@@ -1,8 +1,11 @@
+import functools
 import math
 
 import jax
 import jax.numpy as jnp
 from jax import lax
+from jax.experimental import pallas as pl
+from jax.experimental.pallas import tpu as pltpu
 from jax.sharding import PartitionSpec as P
 
 WIN = 2048
@@ -92,11 +95,304 @@
     return result / total_shots
 
 
+LANES = 128
+HALF = 16
+GROUP = 8
+SLOT = 64
+MESH = pl.DeviceIdType.MESH
+
+
+def lane_fields(shape):
+    lane = lax.broadcasted_iota(jnp.int32, shape, len(shape) - 1)
+    return lane // 32 % 4, lane // 16 % 2, lane % 16
+
+
+def rotated(lag, off_row):
+    freq, part, _ = lane_fields(lag.shape)
+    bins = jnp.full(lag.shape, freq_bins[0], jnp.int32)
+    for f in range(1, len(freq_bins)):
+        bins = jnp.where(freq == f, freq_bins[f], bins)
+    turn = ((lag & (SPACING - 1)) * bins + part * (WIN // 4)) & (WIN - 1)
+    phase = (2.0 * math.pi / WIN) * turn.astype(jnp.float32)
+    return jnp.cos(phase) / math.sqrt(WIN)
+
+
+def kernel(
+    n, off_ref, rec_ref, out_ref,
+    rec, poff, table, tmask, rim_out, rim_in, gat, col, rmat, acc,
+    rec_sem, jit_sem, rim_sem, ring_send, pair_send, chunk_recv, col_send, col_recv,
+):
+    me = lax.axis_index("shot")
+    mj = lax.axis_index("rcv")
+    rows = rec.shape[0]
+    groups = rec.shape[1] // (GROUP * SPACING)
+    span = GROUP * SPACING
+    chips = n // 2
+    nz = chips // 2
+    ncol = col.shape[2]
+    core = me % 2
+    chip = me // 2
+    z, y = chip // 2, chip % 2
+    pos = jnp.where(y == 0, z, chips - 1 - z)
+
+    def device_at(position, which):
+        q = (position + 2 * chips) % chips
+        second = q >= nz
+        zz = jnp.where(second, chips - 1 - q, q)
+        yy = jnp.where(second, 1, 0)
+        return (zz * 2 + yy) * 2 + which
+
+    cw, ccw = device_at(pos + 1, core), device_at(pos - 1, core)
+    pair = chip * 2 + (1 - core)
+    prev, nxt = (me + n - 1) % n, (me + 1) % n
+
+    def load(g):
+        part = pl.ds(g * span, span)
+        return pltpu.make_async_copy(rec_ref.at[:, part], rec.at[:, part], rec_sem.at[g])
+
+    for g in range(groups):
+        load(g).start()
+
+    barrier = pltpu.get_barrier_semaphore()
+    for other in (cw, ccw, pair, prev, nxt):
+        pl.semaphore_signal(barrier, inc=1, device_id=(other, mj), device_id_type=MESH)
+    pl.semaphore_signal(barrier, inc=1, device_id=(me, 1 - mj), device_id_type=MESH)
+    pl.semaphore_wait(barrier, 6)
+
+    jitter = pltpu.make_async_remote_copy(
+        off_ref, poff, jit_sem.at[0], jit_sem.at[1], device_id=(nxt, mj), device_id_type=MESH
+    )
+    jitter.start()
+
+    def lag_of(off_row):
+        u = lax.broadcasted_iota(jnp.int32, (SPACING, LANES), 0)
+        return u - off_row
+
+    def partial_spectra(off_row, groups_of):
+        lag = lag_of(off_row)
+        table[...] = rotated(lag, off_row)
+        total = jnp.zeros((rows, LANES), jnp.float32)
+        for g in groups_of:
+            for b in range(GROUP):
+                here = lag_of(off_row) + (g * GROUP + b) * SPACING
+                inside = (here >= 0) & (here < WIN)
+                tmask[pl.ds(b * SPACING, SPACING), :] = jnp.where(inside, table[...], 0.0).astype(
+                    jnp.bfloat16
+                )
+            total = total + jnp.dot(
+                rec[:, g * span : (g + 1) * span], tmask[...], preferred_element_type=jnp.float32
+            )
+        return total
+
+    def ring(src, h, d):
+        return pltpu.make_async_remote_copy(
+            gat.at[src, h], gat.at[src, h], ring_send.at[d, src, h], chunk_recv.at[src, h],
+            device_id=(cw if d == 0 else ccw, mj), device_id_type=MESH,
+        )
+
+    def share(src, h):
+        return pltpu.make_async_remote_copy(
+            gat.at[src, h], gat.at[src, h], pair_send.at[src, h], chunk_recv.at[src, h],
+            device_id=(pair, mj), device_id_type=MESH,
+        )
+
+    home = me * ncol // rows
+    provider = home == mj
+    first = pl.multiple_of(jnp.where(provider, me * ncol - home * rows, 0), 16)
+
+    def col_far(src, h):
+        return pltpu.make_async_remote_copy(
+            gat.at[src, h, pl.ds(first, ncol), :], col.at[src, h], col_send.at[src, h],
+            col_recv.at[src, h], device_id=(me, 1 - mj), device_id_type=MESH,
+        )
+
+    def col_near(src, h):
+        return pltpu.make_async_copy(
+            gat.at[src, h, pl.ds(first, ncol), :], col.at[src, h], col_recv.at[src, h]
+        )
+
+    def send_col(src, h):
+        @pl.when(provider)
+        def _():
+            col_far(src, h).start()
+            col_near(src, h).start()
+
+    def send_own(h):
+        ring(me, h, 0).start()
+        ring(me, h, 1).start()
+        share(me, h).start()
+        send_col(me, h)
+
+    def gram(src):
+        for h in range(2):
+            x = col[src, h].astype(jnp.float32)
+            freq, part, _ = lane_fields(x.shape)
+            swapped = jnp.where(part == 0, pltpu.roll(x, LANES - 16, 1), -pltpu.roll(x, 16, 1))
+            for ri, value in enumerate((x, swapped)):
+                for f in range(4):
+                    rmat[pl.ds((ri * 4 + f) * SLOT, ncol), h * LANES : (h + 1) * LANES] = jnp.where(
+                        freq == f, value, 0.0
+                    ).astype(jnp.bfloat16)
+        left = jnp.concatenate([gat[src, 0], gat[src, 1]], axis=1)
+        acc[...] += lax.dot_general(
+            left, rmat[...], (((1,), (1,)), ((), ())), preferred_element_type=jnp.float32
+        )
+
+    off0 = off_ref[0:1, 0:LANES]
+    off1 = off_ref[0:1, LANES : 2 * LANES]
+    rmat[...] = jnp.zeros_like(rmat)
+    acc[...] = jnp.zeros_like(acc)
+    for g in range(groups):
+        load(g).wait()
+    gat[me, 0] = partial_spectra(off0, (0, 1, 2)).astype(jnp.bfloat16)
+    send_own(0)
+
+    jitter.wait()
+    offp = poff[0:1, LANES : 2 * LANES] - rec.shape[1]
+    foreign = partial_spectra(offp, (0,))
+    cut = rows // 2
+    rim_out[...] = foreign[:cut] + pltpu.roll(foreign[cut:], LANES - 8, 1)
+    rim = pltpu.make_async_remote_copy(
+        rim_out, rim_in, rim_sem.at[0], rim_sem.at[1], device_id=(prev, mj), device_id_type=MESH
+    )
+    rim.start()
+    second = partial_spectra(off1, (2, 3))
+    rim.wait()
+    _, _, shot = lane_fields((cut, LANES))
+    wanted = (shot >= 8) & (me < n - 1)
+    upper = jnp.where(wanted, rim_in[...], 0.0)
+    lower = jnp.where(wanted, pltpu.roll(rim_in[...], 8, 1), 0.0)
+    gat[me, 1, :cut] = (second[:cut] + upper).astype(jnp.bfloat16)
+    gat[me, 1, cut:] = (second[cut:] + lower).astype(jnp.bfloat16)
+    send_own(1)
+
+    half = chips // 2
+
+    def hops(h, d):
+        return half if h == d else half - 1
+
+    def arrivals(t):
+        found = []
+        for h in range(2):
+            for d in range(2):
+                if 1 <= t <= hops(h, d):
+                    found.append((h, d))
+        return found
+
+    def source(t, d, which):
+        return device_at(pos - t if d == 0 else pos + t, which)
+
+    def step_sources(t):
+        if t == 0:
+            return [0]
+        return [0, 1] if t < half else [0]
+
+    for t in range(half + 1):
+        for h, d in arrivals(t):
+            src = source(t, d, core)
+            ring(src, h, d).wait_recv()
+            if t < hops(h, d):
+                ring(src, h, d).start()
+            share(src, h).start()
+            send_col(src, h)
+        for d in step_sources(t):
+            for h in range(2):
+                src = source(t, d, 1 - core)
+                share(src, h).wait_recv()
+                send_col(src, h)
+        for back in ((t - 1,) if t < half else (t - 1, t)):
+            if back < 0:
+                continue
+            for d in step_sources(back):
+                for which in range(2):
+                    src = source(back, d, which)
+                    for h in range(2):
+                        col_near(src, h).wait()
+                    gram(src)
+
+    scale = 1.0 / (n * 2 * HALF)
+    for g in range(8):
+        out_ref[g // 4, g % 4] = acc[:, g * SLOT : g * SLOT + ncol] * scale
+
+    for h in range(2):
+        ring(me, h, 0).wait_send()
+        ring(me, h, 1).wait_send()
+    for t in range(1, half + 1):
+        for h, d in arrivals(t):
+            src = source(t, d, core)
+            if t < hops(h, d):
+                ring(src, h, d).wait_send()
+            share(src, h).wait_send()
+    for h in range(2):
+        share(me, h).wait_send()
+
+    @pl.when(provider)
+    def _():
+        for src in range(n):
+            for h in range(2):
+                col_far(src, h).wait_send()
+
+
+def fused_device(n, ncol, record, shot_fire_samples):
+    rows, length = record.shape
+    off = shot_fire_samples - lax.axis_index("shot") * length
+    off = jnp.broadcast_to(off.reshape(1, 2, 1, HALF), (8, 2, 8, HALF)).reshape(8, 2 * LANES)
+    return pl.pallas_call(
+        functools.partial(kernel, n),
+        out_shape=jax.ShapeDtypeStruct((2, 4, rows, ncol), jnp.float32),
+        in_specs=[
+            pl.BlockSpec(memory_space=pltpu.VMEM),
+            pl.BlockSpec(memory_space=pl.ANY),
+        ],
+        out_specs=pl.BlockSpec(memory_space=pltpu.VMEM),
+        scratch_shapes=[
+            pltpu.VMEM((rows, length), jnp.bfloat16),
+            pltpu.VMEM((8, 2 * LANES), jnp.int32),
+            pltpu.VMEM((SPACING, LANES), jnp.float32),
+            pltpu.VMEM((GROUP * SPACING, LANES), jnp.bfloat16),
+            pltpu.VMEM((rows // 2, LANES), jnp.float32),
+            pltpu.VMEM((rows // 2, LANES), jnp.float32),
+            pltpu.VMEM((n, 2, rows, LANES), jnp.bfloat16),
+            pltpu.VMEM((n, 2, ncol, LANES), jnp.bfloat16),
+            pltpu.VMEM((8 * SLOT, 2 * LANES), jnp.bfloat16),
+            pltpu.VMEM((rows, 8 * SLOT), jnp.float32),
+            pltpu.SemaphoreType.DMA((length // (GROUP * SPACING),)),
+            pltpu.SemaphoreType.DMA((2,)),
+            pltpu.SemaphoreType.DMA((2,)),
+            pltpu.SemaphoreType.DMA((2, n, 2)),
+            pltpu.SemaphoreType.DMA((n, 2)),
+            pltpu.SemaphoreType.DMA((n, 2)),
+            pltpu.SemaphoreType.DMA((n, 2)),
+            pltpu.SemaphoreType.DMA((n, 2)),
+        ],
+        compiler_params=pltpu.CompilerParams(
+            collective_id=0, has_side_effects=True, vmem_limit_bytes=40 * 1024 * 1024
+        ),
+    )(off, record)
+
+
+def whole_step(n, receivers, record, shot_fire_samples):
+    rows, length = record.shape
+    shots = shot_fire_samples.shape[0]
+    ncol = receivers // n
+    fits = (
+        receivers == 2 * rows and ncol % 16 == 0 and ncol <= SLOT and rows % (2 * ncol) == 0
+        and shots == 2 * HALF and length == shots * SPACING and n % 8 == 0
+    )
+    if fits:
+        return fused_device(n, ncol, record, shot_fire_samples)
+    return per_device(record, shot_fire_samples)
+
+
 def solution(mesh):
-    return jax.shard_map(
-        per_device,
-        mesh=mesh,
-        in_specs=(P("rcv", "shot"), P("shot")),
-        out_specs=P(None, None, "rcv", "shot"),
-        check_vma=False,
-    )
+    def step(record, shot_fire_samples):
+        body = functools.partial(whole_step, mesh.shape["shot"], record.shape[0])
+        return jax.shard_map(
+            body,
+            mesh=mesh,
+            in_specs=(P("rcv", "shot"), P("shot")),
+            out_specs=P(None, None, "rcv", "shot"),
+            check_vma=False,
+        )(record, shot_fire_samples)
+
+    return step

time: 126 us -> 39.8 us (0.32)
  blocking collectives: 36.5 us -> 0 us
  Pallas kernels: 0 us -> 34.5 us
  other arithmetic: 26.6 us -> 0.66 us
  waiting for transfers between devices: 17 us -> 0 us
  local copies, waits for them, and re-layouts: 20.2 us -> 4.23 us
  between operations: 13.6 us -> 0.01 us
  matrix products: 10.5 us -> 0 us
  starting transfers between devices: 1.29 us -> 0 us
    pallas_call x0 -> x1, Pallas kernels: none -> 34.5 us  [fused_device(): pl.pallas_call(functools.partial(kernel, n), out_shape=jax.ShapeDtypeStru...]
    all_to_all x1 -> x0, blocking collectives: 28.9 us -> none  [per_device(): lax.all_to_all(all_receivers, 'shot', split_axis=2, concat_axis=0, tiled=...]
    all_gather x1 -> x0, waiting for transfers between devices: 16.9 us -> none  [per_device(): row_side = lax.all_gather(trace_spectra, 'shot', axis=0, tiled=True)]
    concatenate x1 -> x0, other arithmetic: 14.8 us -> none  [per_device(): extended = jnp.concatenate([record, rim_rows], axis=1)]
    dot_general x13 -> x0, matrix products: 10.5 us -> none  [the longest x9 9.03 us: local_spectra(): jnp.einsum('rsu,scu->scr', record_part, tables[:, :, offset, :], preferre...]
    cos x1 -> x0, other arithmetic: 9.74 us -> none  [shifted_tables(): jnp.cos(phase_angle)]
    unnamed x9 -> x2, local copies, waits for them, and re-layouts: 10.9 us -> 2.79 us
    all_gather x1 -> x0, blocking collectives: 7.55 us -> none  [per_device(): all_receivers = lax.all_gather(trace_spectra, 'rcv', axis=2, tiled=True)]
  transfers between devices with their start and end apart: 2 -> 0, of which waited for: 1 -> 0; matrix products, arithmetic and copies ran while one was open for 12% -> 0% of each run, Pallas kernels for 0% -> 0%
where the time goes in v1:
time: 39.8 us; the launch traced here: 39.4 us
  Pallas kernels  34.5 us (87%)
  local copies, waits for them, and re-layouts  4.23 us (11%)
  other arithmetic  0.66 us (2%)
    pallas_call x1, Pallas kernels, fused_device(): pl.pallas_call(functools.partial(kernel, n), out_shape=jax.ShapeDtypeStru...  34.5 us
    unnamed x2, local copies, waits for them, and re-layouts  2.79 us
    pallas_call x1, local copies, waits for them, and re-layouts, fused_device(): pl.pallas_call(functools.partial(kernel, n), out_shape=jax.ShapeDtypeStru...  1.27 us

profile of v1, /device:TPU:0, one launch (start us, length us, event | category | flops | bytes accessed | tf_op | source)
XLA Modules:
  0.0 39.4 jit_solution(13098399503386137140)
XLA Ops:
  0.0 0.7 %broadcast_subtract_fusion = s32[32]{0:T(128)S(1)} fusion(s32[32]{0:T(128)} %param.3, s32[]{:T(128)S(6)} %mul.3), kind=kLoop, calls=%fused_computation | loop fusion | flops 32 | bytes 260 | tf_op jit(solution)/shard_map/sub | solution.py:338
  0.7 0.1 broadcast_in_dim.11
  0.7 0.1 broadcast_in_dim.13
  0.8 0.0 copy-start
  0.8 2.8 %copy-done = bf16[384,8192]{1,0:T(8,128)(2,1)S(1)} copy-done((bf16[384,8192]{1,0:T(8,128)(2,1)S(1)}, bf16[384,8192]{1,0:T(8,128)(2,1)}, u32[]{:S(2)}) %copy-start) | copy-done | bytes 6291480
  3.6 34.5 %shard_map.28 = f32[2,4,384,48]{3,2,1,0:T(8,128)S(1)} custom-call(s32[8,256]{1,0:T(8,128)S(1)} %broadcast_in_dim.14.off_ref, bf16[384,8192]{1,0:T(8,128)(2,1)S(1)} %copy-done), custom_call_target="tpu_custom_call" | custom-call | tf_op jit(solution)/shard_map/pallas_call | solution.py:340
  38.1 1.3 %copy.3 = f32[2,4,384,48]{2,3,1,0:T(8,128)} copy(f32[2,4,384,48]{3,2,1,0:T(8,128)S(1)} %shard_map.28) | data formatting | bytes 1179648 | tf_op jit(solution)/shard_map/pallas_call | solution.py:340
  (2 shorter events, 0.0 us)
Async XLA Ops:
  0.8 2.8 %copy-start = (bf16[384,8192]{1,0:T(8,128)(2,1)S(1)}, bf16[384,8192]{1,0:T(8,128)(2,1)}, u32[]{:S(2)}) copy-start(bf16[384,8192]{1,0:T(8,128)(2,1)} %rec_ref.1) | copy-start | bytes 18874372

commit v2 on v1

--- a/solution.py
+++ b/solution.py
@@ -98,7 +98,6 @@
 LANES = 128
 HALF = 16
 GROUP = 8
-SLOT = 64
 MESH = pl.DeviceIdType.MESH
 
 
@@ -118,8 +117,8 @@
 
 
 def kernel(
-    n, off_ref, rec_ref, out_ref,
-    rec, poff, table, tmask, rim_out, rim_in, gat, col, rmat, acc,
+    n, fire_ref, rec_ref, out_ref,
+    rec, joff, poff, table, tmask, rim_out, rim_in, gat, col, rmat, acc,
     rec_sem, jit_sem, rim_sem, ring_send, pair_send, chunk_recv, col_send, col_recv,
 ):
     me = lax.axis_index("shot")
@@ -153,6 +152,15 @@
     for g in range(groups):
         load(g).start()
 
+    _, _, shot_lane = lane_fields((1, LANES))
+    offs = []
+    for h in range(2):
+        row = jnp.zeros((1, LANES), jnp.int32)
+        for s in range(HALF):
+            row = jnp.where(shot_lane == s, fire_ref[h * HALF + s], row)
+        offs.append(row - me * rec.shape[1])
+    joff[...] = jnp.broadcast_to(offs[1], joff.shape)
+
     barrier = pltpu.get_barrier_semaphore()
     for other in (cw, ccw, pair, prev, nxt):
         pl.semaphore_signal(barrier, inc=1, device_id=(other, mj), device_id_type=MESH)
@@ -160,7 +168,7 @@
     pl.semaphore_wait(barrier, 6)
 
     jitter = pltpu.make_async_remote_copy(
-        off_ref, poff, jit_sem.at[0], jit_sem.at[1], device_id=(nxt, mj), device_id_type=MESH
+        joff, poff, jit_sem.at[0], jit_sem.at[1], device_id=(nxt, mj), device_id_type=MESH
     )
     jitter.start()
 
@@ -168,11 +176,13 @@
         u = lax.broadcasted_iota(jnp.int32, (SPACING, LANES), 0)
         return u - off_row
 
-    def partial_spectra(off_row, groups_of):
+    def partial_spectra(off_row, groups_of, fresh=()):
         lag = lag_of(off_row)
         table[...] = rotated(lag, off_row)
         total = jnp.zeros((rows, LANES), jnp.float32)
         for g in groups_of:
+            if g in fresh:
+                load(g).wait()
             for b in range(GROUP):
                 here = lag_of(off_row) + (g * GROUP + b) * SPACING
                 inside = (here >= 0) & (here < WIN)
@@ -230,25 +240,20 @@
             swapped = jnp.where(part == 0, pltpu.roll(x, LANES - 16, 1), -pltpu.roll(x, 16, 1))
             for ri, value in enumerate((x, swapped)):
                 for f in range(4):
-                    rmat[pl.ds((ri * 4 + f) * SLOT, ncol), h * LANES : (h + 1) * LANES] = jnp.where(
+                    rmat[pl.ds((ri * 4 + f) * ncol, ncol), h * LANES : (h + 1) * LANES] = jnp.where(
                         freq == f, value, 0.0
                     ).astype(jnp.bfloat16)
         left = jnp.concatenate([gat[src, 0], gat[src, 1]], axis=1)
         acc[...] += lax.dot_general(
-            left, rmat[...], (((1,), (1,)), ((), ())), preferred_element_type=jnp.float32
-        )
-
-    off0 = off_ref[0:1, 0:LANES]
-    off1 = off_ref[0:1, LANES : 2 * LANES]
-    rmat[...] = jnp.zeros_like(rmat)
+            rmat[...], left, (((1,), (1,)), ((), ())), preferred_element_type=jnp.float32
+        )
+
     acc[...] = jnp.zeros_like(acc)
-    for g in range(groups):
-        load(g).wait()
-    gat[me, 0] = partial_spectra(off0, (0, 1, 2)).astype(jnp.bfloat16)
+    gat[me, 0] = partial_spectra(offs[0], (0, 1, 2), (0, 1, 2)).astype(jnp.bfloat16)
     send_own(0)
 
     jitter.wait()
-    offp = poff[0:1, LANES : 2 * LANES] - rec.shape[1]
+    offp = poff[0:1, :] - rec.shape[1]
     foreign = partial_spectra(offp, (0,))
     cut = rows // 2
     rim_out[...] = foreign[:cut] + pltpu.roll(foreign[cut:], LANES - 8, 1)
@@ -256,7 +261,7 @@
         rim_out, rim_in, rim_sem.at[0], rim_sem.at[1], device_id=(prev, mj), device_id_type=MESH
     )
     rim.start()
-    second = partial_spectra(off1, (2, 3))
+    second = partial_spectra(offs[1], (2, 3), (3,))
     rim.wait()
     _, _, shot = lane_fields((cut, LANES))
     wanted = (shot >= 8) & (me < n - 1)
@@ -287,6 +292,14 @@
             return [0]
         return [0, 1] if t < half else [0]
 
+    def gram_step(t):
+        for which in (core, 1 - core):
+            for d in step_sources(t):
+                src = source(t, d, which)
+                for h in range(2):
+                    col_near(src, h).wait()
+                gram(src)
+
     for t in range(half + 1):
         for h, d in arrivals(t):
             src = source(t, d, core)
@@ -295,24 +308,18 @@
                 ring(src, h, d).start()
             share(src, h).start()
             send_col(src, h)
+        if t > 0:
+            gram_step(t - 1)
         for d in step_sources(t):
             for h in range(2):
                 src = source(t, d, 1 - core)
                 share(src, h).wait_recv()
                 send_col(src, h)
-        for back in ((t - 1,) if t < half else (t - 1, t)):
-            if back < 0:
-                continue
-            for d in step_sources(back):
-                for which in range(2):
-                    src = source(back, d, which)
-                    for h in range(2):
-                        col_near(src, h).wait()
-                    gram(src)
+    gram_step(half)
 
     scale = 1.0 / (n * 2 * HALF)
     for g in range(8):
-        out_ref[g // 4, g % 4] = acc[:, g * SLOT : g * SLOT + ncol] * scale
+        out_ref[g // 4, g % 4] = acc[g * ncol : (g + 1) * ncol, :] * scale
 
     for h in range(2):
         ring(me, h, 0).wait_send()
@@ -335,27 +342,26 @@
 
 def fused_device(n, ncol, record, shot_fire_samples):
     rows, length = record.shape
-    off = shot_fire_samples - lax.axis_index("shot") * length
-    off = jnp.broadcast_to(off.reshape(1, 2, 1, HALF), (8, 2, 8, HALF)).reshape(8, 2 * LANES)
-    return pl.pallas_call(
+    gram = pl.pallas_call(
         functools.partial(kernel, n),
-        out_shape=jax.ShapeDtypeStruct((2, 4, rows, ncol), jnp.float32),
+        out_shape=jax.ShapeDtypeStruct((2, 4, ncol, rows), jnp.float32),
         in_specs=[
-            pl.BlockSpec(memory_space=pltpu.VMEM),
+            pl.BlockSpec(memory_space=pltpu.SMEM),
             pl.BlockSpec(memory_space=pl.ANY),
         ],
         out_specs=pl.BlockSpec(memory_space=pltpu.VMEM),
         scratch_shapes=[
             pltpu.VMEM((rows, length), jnp.bfloat16),
-            pltpu.VMEM((8, 2 * LANES), jnp.int32),
+            pltpu.VMEM((8, LANES), jnp.int32),
+            pltpu.VMEM((8, LANES), jnp.int32),
             pltpu.VMEM((SPACING, LANES), jnp.float32),
             pltpu.VMEM((GROUP * SPACING, LANES), jnp.bfloat16),
             pltpu.VMEM((rows // 2, LANES), jnp.float32),
             pltpu.VMEM((rows // 2, LANES), jnp.float32),
             pltpu.VMEM((n, 2, rows, LANES), jnp.bfloat16),
             pltpu.VMEM((n, 2, ncol, LANES), jnp.bfloat16),
-            pltpu.VMEM((8 * SLOT, 2 * LANES), jnp.bfloat16),
-            pltpu.VMEM((rows, 8 * SLOT), jnp.float32),
+            pltpu.VMEM((8 * ncol, 2 * LANES), jnp.bfloat16),
+            pltpu.VMEM((8 * ncol, rows), jnp.float32),
             pltpu.SemaphoreType.DMA((length // (GROUP * SPACING),)),
             pltpu.SemaphoreType.DMA((2,)),
             pltpu.SemaphoreType.DMA((2,)),
@@ -366,9 +372,10 @@
             pltpu.SemaphoreType.DMA((n, 2)),
         ],
         compiler_params=pltpu.CompilerParams(
-            collective_id=0, has_side_effects=True, vmem_limit_bytes=40 * 1024 * 1024
+            collective_id=0, has_side_effects=True, vmem_limit_bytes=59 * 1024 * 1024
         ),
-    )(off, record)
+    )(shot_fire_samples, record)
+    return gram.transpose(0, 1, 3, 2)
 
 
 def whole_step(n, receivers, record, shot_fire_samples):
@@ -376,7 +383,7 @@
     shots = shot_fire_samples.shape[0]
     ncol = receivers // n
     fits = (
-        receivers == 2 * rows and ncol % 16 == 0 and ncol <= SLOT and rows % (2 * ncol) == 0
+        receivers == 2 * rows and ncol % 16 == 0 and rows % (2 * ncol) == 0
         and shots == 2 * HALF and length == shots * SPACING and n % 8 == 0
     )
     if fits:

time: 39.8 us -> 37.9 us (0.952)
  local copies, waits for them, and re-layouts: 4.23 us -> 1.92 us
  Pallas kernels: 34.5 us -> 35.5 us
  other arithmetic: 0.66 us -> 0 us
    pallas_call x1 -> x0, local copies, waits for them, and re-layouts: 1.27 us -> none  [fused_device(): pl.pallas_call(functools.partial(kernel, n), out_shape=jax.ShapeDtypeStru...]
    pallas_call x1, Pallas kernels: 34.5 us -> 35.5 us  [fused_device(): pl.pallas_call(functools.partial(kernel, n), out_shape=jax.ShapeDtypeStru...]
    unnamed x2 -> x1, local copies, waits for them, and re-layouts: 2.79 us -> 1.92 us
    sub x1 -> x0, other arithmetic: 0.66 us -> none  [fused_device(): off = shot_fire_samples - lax.axis_index('shot') * length]
where the time goes in v2:
time: 37.9 us; the launch traced here: 37.5 us
  Pallas kernels  35.5 us (94%)
  local copies, waits for them, and re-layouts  1.92 us (5%)
    pallas_call x1, Pallas kernels, fused_device(): pl.pallas_call(functools.partial(kernel, n), out_shape=jax.ShapeDtypeStru...  35.5 us
    unnamed x1, local copies, waits for them, and re-layouts  1.92 us

profile of v2, /device:TPU:0, one launch (start us, length us, event | category | flops | bytes accessed | tf_op | source)
XLA Modules:
  0.0 37.5 jit_solution(12964240732666768349)
XLA Ops:
  0.0 35.5 %shard_map.28 = f32[2,4,48,384]{3,2,1,0:T(8,128)} custom-call(s32[32]{0:T(128)} %fire_ref.1, bf16[384,8192]{1,0:T(8,128)(2,1)} %rec_ref.1), custom_call_target="tpu_custom_call" | custom-call | tf_op jit(solution)/shard_map/pallas_call | solution.py:345
  35.5 1.9 %copy.4 = f32[2,4,384,48]{2,3,1,0:T(8,128)} copy(f32[2,4,384,48]{2,3,1,0:T(8,128)} %bitcast.1) | data formatting | bytes 1179648

commit v3 on v2

--- a/solution.py
+++ b/solution.py
@@ -106,14 +106,20 @@
     return lane // 32 % 4, lane // 16 % 2, lane % 16
 
 
-def rotated(lag, off_row):
-    freq, part, _ = lane_fields(lag.shape)
-    bins = jnp.full(lag.shape, freq_bins[0], jnp.int32)
+def rotated(lag):
+    freq, part, _ = lane_fields((1, LANES))
+    bins = jnp.full((1, LANES), freq_bins[0], jnp.int32)
     for f in range(1, len(freq_bins)):
         bins = jnp.where(freq == f, freq_bins[f], bins)
-    turn = ((lag & (SPACING - 1)) * bins + part * (WIN // 4)) & (WIN - 1)
-    phase = (2.0 * math.pi / WIN) * turn.astype(jnp.float32)
-    return jnp.cos(phase) / math.sqrt(WIN)
+    turn = (lag & (SPACING - 1)) * bins + part * (WIN // 4)
+    turn = ((turn + WIN // 2) & (WIN - 1)) - WIN // 2
+    x = (math.pi / WIN) * turn.astype(jnp.float32)
+    y = x * x
+    series = 1.0 / math.factorial(13)
+    for k in (11, 9, 7, 5, 3, 1):
+        series = series * y + (-1.0) ** (k // 2) / math.factorial(k)
+    half_sine = x * series
+    return (1.0 - 2.0 * half_sine * half_sine) / math.sqrt(WIN)
 
 
 def kernel(
@@ -124,11 +130,11 @@
     me = lax.axis_index("shot")
     mj = lax.axis_index("rcv")
     rows = rec.shape[0]
-    groups = rec.shape[1] // (GROUP * SPACING)
     span = GROUP * SPACING
     chips = n // 2
     nz = chips // 2
     ncol = col.shape[2]
+    shift, reach = SPACING.bit_length() - 1, WIN // SPACING
     core = me % 2
     chip = me // 2
     z, y = chip // 2, chip % 2
@@ -149,7 +155,7 @@
         part = pl.ds(g * span, span)
         return pltpu.make_async_copy(rec_ref.at[:, part], rec.at[:, part], rec_sem.at[g])
 
-    for g in range(groups):
+    for g in (1, 2, 0, 3):
         load(g).start()
 
     _, _, shot_lane = lane_fields((1, LANES))
@@ -172,27 +178,28 @@
     )
     jitter.start()
 
-    def lag_of(off_row):
+    def fill_tables(kind, off_row):
         u = lax.broadcasted_iota(jnp.int32, (SPACING, LANES), 0)
-        return u - off_row
-
-    def partial_spectra(off_row, groups_of, fresh=()):
-        lag = lag_of(off_row)
-        table[...] = rotated(lag, off_row)
-        total = jnp.zeros((rows, LANES), jnp.float32)
-        for g in groups_of:
-            if g in fresh:
-                load(g).wait()
+        start = off_row & (SPACING - 1)
+        value = rotated(u - start)
+        table[kind, 0] = jnp.where(u >= start, value, 0.0).astype(jnp.bfloat16)
+        table[kind, 1] = jnp.where(u < start, value, 0.0).astype(jnp.bfloat16)
+
+    def group_dot(g, kinds):
+        for slot, (kind, off_row) in enumerate(kinds):
+            block_of = jnp.broadcast_to(off_row >> shift, (16, LANES))
+            lanes = slice(slot * LANES, (slot + 1) * LANES)
             for b in range(GROUP):
-                here = lag_of(off_row) + (g * GROUP + b) * SPACING
-                inside = (here >= 0) & (here < WIN)
-                tmask[pl.ds(b * SPACING, SPACING), :] = jnp.where(inside, table[...], 0.0).astype(
-                    jnp.bfloat16
-                )
-            total = total + jnp.dot(
-                rec[:, g * span : (g + 1) * span], tmask[...], preferred_element_type=jnp.float32
-            )
-        return total
+                order = g * GROUP + b - block_of
+                early = ((order >= 0) & (order < reach)).astype(jnp.float32).astype(jnp.bfloat16)
+                late = ((order >= 1) & (order <= reach)).astype(jnp.float32).astype(jnp.bfloat16)
+                block = (SPACING // 16, 16, LANES)
+                mixed = table[kind, 0].reshape(block) * early + table[kind, 1].reshape(block) * late
+                tmask[b * SPACING : (b + 1) * SPACING, lanes] = mixed.reshape(SPACING, LANES)
+        return jnp.dot(
+            rec[:, g * span : (g + 1) * span], tmask[:, : len(kinds) * LANES],
+            preferred_element_type=jnp.float32,
+        )
 
     def ring(src, h, d):
         return pltpu.make_async_remote_copy(
@@ -248,20 +255,30 @@
             rmat[...], left, (((1,), (1,)), ((), ())), preferred_element_type=jnp.float32
         )
 
+    fill_tables(0, offs[0])
+    fill_tables(1, offs[1])
     acc[...] = jnp.zeros_like(acc)
-    gat[me, 0] = partial_spectra(offs[0], (0, 1, 2), (0, 1, 2)).astype(jnp.bfloat16)
-    send_own(0)
-
+    kinds = ((0, offs[0]), (1, offs[1]))
+    load(1).wait()
+    own = group_dot(1, kinds[:1])
+    load(2).wait()
+    both = group_dot(2, kinds)
     jitter.wait()
     offp = poff[0:1, :] - rec.shape[1]
-    foreign = partial_spectra(offp, (0,))
+    fill_tables(2, offp)
+    load(0).wait()
+    head = group_dot(0, (kinds[0], (2, offp)))
+    gat[me, 0] = (own + both[:, :LANES] + head[:, :LANES]).astype(jnp.bfloat16)
+    send_own(0)
+    foreign = head[:, LANES:]
     cut = rows // 2
     rim_out[...] = foreign[:cut] + pltpu.roll(foreign[cut:], LANES - 8, 1)
     rim = pltpu.make_async_remote_copy(
         rim_out, rim_in, rim_sem.at[0], rim_sem.at[1], device_id=(prev, mj), device_id_type=MESH
     )
     rim.start()
-    second = partial_spectra(offs[1], (2, 3), (3,))
+    load(3).wait()
+    second = both[:, LANES:] + group_dot(3, kinds[1:])
     rim.wait()
     _, _, shot = lane_fields((cut, LANES))
     wanted = (shot >= 8) & (me < n - 1)
@@ -354,8 +371,8 @@
             pltpu.VMEM((rows, length), jnp.bfloat16),
             pltpu.VMEM((8, LANES), jnp.int32),
             pltpu.VMEM((8, LANES), jnp.int32),
-            pltpu.VMEM((SPACING, LANES), jnp.float32),
-            pltpu.VMEM((GROUP * SPACING, LANES), jnp.bfloat16),
+            pltpu.VMEM((3, 2, SPACING, LANES), jnp.bfloat16),
+            pltpu.VMEM((GROUP * SPACING, 2 * LANES), jnp.bfloat16),
             pltpu.VMEM((rows // 2, LANES), jnp.float32),
             pltpu.VMEM((rows // 2, LANES), jnp.float32),
             pltpu.VMEM((n, 2, rows, LANES), jnp.bfloat16),
@@ -372,7 +389,7 @@
             pltpu.SemaphoreType.DMA((n, 2)),
         ],
         compiler_params=pltpu.CompilerParams(
-            collective_id=0, has_side_effects=True, vmem_limit_bytes=59 * 1024 * 1024
+            collective_id=0, has_side_effects=True, vmem_limit_bytes=56 * 1024 * 1024
         ),
     )(shot_fire_samples, record)
     return gram.transpose(0, 1, 3, 2)

time: 37.9 us -> 38.5 us (1.016)
  Pallas kernels: 35.5 us -> 36 us
    pallas_call x1, Pallas kernels: 35.5 us -> 36 us  [fused_device(): pl.pallas_call(functools.partial(kernel, n), out_shape=jax.ShapeDtypeStru...]
where the time goes in v3:
time: 38.5 us; the launch traced here: 37.9 us
  Pallas kernels  36 us (94%)
  local copies, waits for them, and re-layouts  1.92 us (5%)
    pallas_call x1, Pallas kernels, fused_device(): pl.pallas_call(functools.partial(kernel, n), out_shape=jax.ShapeDtypeStru...  36 us
    unnamed x1, local copies, waits for them, and re-layouts  1.92 us

profile of v3, /device:TPU:0, one launch (start us, length us, event | category | flops | bytes accessed | tf_op | source)
XLA Modules:
  0.0 37.9 jit_solution(4621820128802909223)
XLA Ops:
  0.0 36.0 %shard_map.28 = f32[2,4,48,384]{3,2,1,0:T(8,128)} custom-call(s32[32]{0:T(128)} %fire_ref.1, bf16[384,8192]{1,0:T(8,128)(2,1)} %rec_ref.1), custom_call_target="tpu_custom_call" | custom-call | tf_op jit(solution)/shard_map/pallas_call | solution.py:362
  36.0 1.9 %copy.4 = f32[2,4,384,48]{2,3,1,0:T(8,128)} copy(f32[2,4,384,48]{2,3,1,0:T(8,128)} %bitcast.1) | data formatting | bytes 1179648

commit v4 on v3

--- a/solution.py
+++ b/solution.py
@@ -123,8 +123,8 @@
 
 
 def kernel(
-    n, fire_ref, rec_ref, out_ref,
-    rec, joff, poff, table, tmask, rim_out, rim_in, gat, col, rmat, acc,
+    n, fire_hbm, rec_ref, out_ref,
+    fire_ref, fire_sem, rec, joff, poff, table, tmask, rim_out, rim_in, gat, col, rmat, acc,
     rec_sem, jit_sem, rim_sem, ring_send, pair_send, chunk_recv, col_send, col_recv,
 ):
     me = lax.axis_index("shot")
@@ -155,9 +155,16 @@
         part = pl.ds(g * span, span)
         return pltpu.make_async_copy(rec_ref.at[:, part], rec.at[:, part], rec_sem.at[g])
 
+    fires = pltpu.make_async_copy(fire_hbm, fire_ref, fire_sem)
+    fires.start()
     for g in (1, 2, 0, 3):
         load(g).start()
 
+    barrier = pltpu.get_barrier_semaphore()
+    for other in (cw, ccw, pair, prev, nxt):
+        pl.semaphore_signal(barrier, inc=1, device_id=(other, mj), device_id_type=MESH)
+    pl.semaphore_signal(barrier, inc=1, device_id=(me, 1 - mj), device_id_type=MESH)
+    fires.wait()
     _, _, shot_lane = lane_fields((1, LANES))
     offs = []
     for h in range(2):
@@ -167,16 +174,9 @@
         offs.append(row - me * rec.shape[1])
     joff[...] = jnp.broadcast_to(offs[1], joff.shape)
 
-    barrier = pltpu.get_barrier_semaphore()
-    for other in (cw, ccw, pair, prev, nxt):
-        pl.semaphore_signal(barrier, inc=1, device_id=(other, mj), device_id_type=MESH)
-    pl.semaphore_signal(barrier, inc=1, device_id=(me, 1 - mj), device_id_type=MESH)
-    pl.semaphore_wait(barrier, 6)
-
     jitter = pltpu.make_async_remote_copy(
         joff, poff, jit_sem.at[0], jit_sem.at[1], device_id=(nxt, mj), device_id_type=MESH
     )
-    jitter.start()
 
     def fill_tables(kind, off_row):
         u = lax.broadcasted_iota(jnp.int32, (SPACING, LANES), 0)
@@ -261,16 +261,18 @@
     kinds = ((0, offs[0]), (1, offs[1]))
     load(1).wait()
     own = group_dot(1, kinds[:1])
+    pl.semaphore_wait(barrier, 6)
+    jitter.start()
     load(2).wait()
     both = group_dot(2, kinds)
+    load(0).wait()
+    own = own + both[:, :LANES] + group_dot(0, kinds[:1])
+    gat[me, 0] = own.astype(jnp.bfloat16)
+    send_own(0)
     jitter.wait()
     offp = poff[0:1, :] - rec.shape[1]
     fill_tables(2, offp)
-    load(0).wait()
-    head = group_dot(0, (kinds[0], (2, offp)))
-    gat[me, 0] = (own + both[:, :LANES] + head[:, :LANES]).astype(jnp.bfloat16)
-    send_own(0)
-    foreign = head[:, LANES:]
+    foreign = group_dot(0, ((2, offp),))
     cut = rows // 2
     rim_out[...] = foreign[:cut] + pltpu.roll(foreign[cut:], LANES - 8, 1)
     rim = pltpu.make_async_remote_copy(
@@ -363,11 +365,13 @@
         functools.partial(kernel, n),
         out_shape=jax.ShapeDtypeStruct((2, 4, ncol, rows), jnp.float32),
         in_specs=[
-            pl.BlockSpec(memory_space=pltpu.SMEM),
-            pl.BlockSpec(memory_space=pl.ANY),
+            pl.BlockSpec(memory_space=pltpu.HBM),
+            pl.BlockSpec(memory_space=pltpu.HBM),
         ],
         out_specs=pl.BlockSpec(memory_space=pltpu.VMEM),
         scratch_shapes=[
+            pltpu.SMEM(shot_fire_samples.shape, jnp.int32),
+            pltpu.SemaphoreType.DMA,
             pltpu.VMEM((rows, length), jnp.bfloat16),
             pltpu.VMEM((8, LANES), jnp.int32),
             pltpu.VMEM((8, LANES), jnp.int32),
@@ -389,7 +393,7 @@
             pltpu.SemaphoreType.DMA((n, 2)),
         ],
         compiler_params=pltpu.CompilerParams(
-            collective_id=0, has_side_effects=True, vmem_limit_bytes=56 * 1024 * 1024
+            collective_id=0, has_side_effects=True, vmem_limit_bytes=50 * 1024 * 1024
         ),
     )(shot_fire_samples, record)
     return gram.transpose(0, 1, 3, 2)

time: 38.5 us -> 35.1 us (0.912)
  Pallas kernels: 36 us -> 32.9 us
  local copies, waits for them, and re-layouts: 1.92 us -> 1.47 us
    pallas_call x1, Pallas kernels: 36 us -> 32.9 us  [fused_device(): pl.pallas_call(functools.partial(kernel, n), out_shape=jax.ShapeDtypeStru...]
    unnamed x1 -> x3, local copies, waits for them, and re-layouts: 1.92 us -> 1.47 us
where the time goes in v4:
time: 35.1 us; the launch traced here: 34.4 us
  Pallas kernels  32.9 us (94%)
  local copies, waits for them, and re-layouts  1.47 us (4%)
    pallas_call x1, Pallas kernels, fused_device(): pl.pallas_call(functools.partial(kernel, n), out_shape=jax.ShapeDtypeStru...  32.9 us
    unnamed x3, local copies, waits for them, and re-layouts  1.47 us

profile of v4, /device:TPU:0, one launch (start us, length us, event | category | flops | bytes accessed | tf_op | source)
XLA Modules:
  0.0 34.4 jit_solution(16330310114408834829)
XLA Ops:
  0.0 0.0 copy-start
  0.0 0.7 %copy-done = s32[32]{0:T(128)S(1)} copy-done((s32[32]{0:T(128)S(1)}, s32[32]{0:T(128)}, u32[]{:S(2)}) %copy-start) | copy-done | bytes 152
  0.7 32.9 %shard_map.28 = f32[2,4,48,384]{3,2,1,0:T(8,128)S(1)} custom-call(s32[32]{0:T(128)S(1)} %copy-done, bf16[384,8192]{1,0:T(8,128)(2,1)} %rec_ref.1), custom_call_target="tpu_custom_call" | custom-call | tf_op jit(solution)/shard_map/pallas_call | solution.py:364
  33.6 0.8 %copy.4 = f32[2,4,384,48]{2,3,1,0:T(8,128)} copy(f32[2,4,384,48]{2,3,1,0:T(8,128)S(1)} %bitcast.1) | data formatting | bytes 1179648
Async XLA Ops:
  0.0 0.7 %copy-start = (s32[32]{0:T(128)S(1)}, s32[32]{0:T(128)}, u32[]{:S(2)}) copy-start(s32[32]{0:T(128)} %fire_hbm.1) | copy-start | bytes 388

commit v5 on v4

--- a/solution.py
+++ b/solution.py
@@ -254,6 +254,52 @@
         acc[...] += lax.dot_general(
             rmat[...], left, (((1,), (1,)), ((), ())), preferred_element_type=jnp.float32
         )
+
+    half = chips // 2
+
+    def hops(h, d):
+        return half if h == d else half - 1
+
+    def arrivals(t):
+        found = []
+        for h in range(2):
+            for d in range(2):
+                if 1 <= t <= hops(h, d):
+                    found.append((h, d))
+        return found
+
+    def source(t, d, which):
+        return device_at(pos - t if d == 0 else pos + t, which)
+
+    def step_sources(t):
+        if t == 0:
+            return [0]
+        return [0, 1] if t < half else [0]
+
+    def gram_step(t):
+        for which in (core, 1 - core):
+            for d in step_sources(t):
+                src = source(t, d, which)
+                for h in range(2):
+                    col_near(src, h).wait()
+                gram(src)
+
+    def ring_stage(h, t):
+        for hh, d in arrivals(t):
+            if hh == h:
+                src = source(t, d, core)
+                ring(src, h, d).wait_recv()
+                if t < hops(h, d):
+                    ring(src, h, d).start()
+                share(src, h).start()
+                send_col(src, h)
+
+    def pair_stage(h, t):
+        ways = [0] if t == 0 else [d for hh, d in arrivals(t) if hh == h]
+        for d in ways:
+            src = source(t, d, 1 - core)
+            share(src, h).wait_recv()
+            send_col(src, h)
 
     fill_tables(0, offs[0])
     fill_tables(1, offs[1])
@@ -281,6 +327,7 @@
     rim.start()
     load(3).wait()
     second = both[:, LANES:] + group_dot(3, kinds[1:])
+    ring_stage(0, 1)
     rim.wait()
     _, _, shot = lane_fields((cut, LANES))
     wanted = (shot >= 8) & (me < n - 1)
@@ -290,50 +337,14 @@
     gat[me, 1, cut:] = (second[cut:] + lower).astype(jnp.bfloat16)
     send_own(1)
 
-    half = chips // 2
-
-    def hops(h, d):
-        return half if h == d else half - 1
-
-    def arrivals(t):
-        found = []
-        for h in range(2):
-            for d in range(2):
-                if 1 <= t <= hops(h, d):
-                    found.append((h, d))
-        return found
-
-    def source(t, d, which):
-        return device_at(pos - t if d == 0 else pos + t, which)
-
-    def step_sources(t):
-        if t == 0:
-            return [0]
-        return [0, 1] if t < half else [0]
-
-    def gram_step(t):
-        for which in (core, 1 - core):
-            for d in step_sources(t):
-                src = source(t, d, which)
-                for h in range(2):
-                    col_near(src, h).wait()
-                gram(src)
-
-    for t in range(half + 1):
-        for h, d in arrivals(t):
-            src = source(t, d, core)
-            ring(src, h, d).wait_recv()
-            if t < hops(h, d):
-                ring(src, h, d).start()
-            share(src, h).start()
-            send_col(src, h)
-        if t > 0:
-            gram_step(t - 1)
-        for d in step_sources(t):
-            for h in range(2):
-                src = source(t, d, 1 - core)
-                share(src, h).wait_recv()
-                send_col(src, h)
+    pair_stage(0, 0)
+    for t in range(1, half + 1):
+        ring_stage(0, t + 1)
+        ring_stage(1, t)
+        pair_stage(0, t)
+        pair_stage(1, t - 1)
+        gram_step(t - 1)
+    pair_stage(1, half)
     gram_step(half)
 
     scale = 1.0 / (n * 2 * HALF)

time: 35.1 us -> 36.4 us (1.037); the launches traced: 34.4 us -> 36.2 us
  Pallas kernels: 32.9 us -> 34.7 us
    pallas_call x1, Pallas kernels: 32.9 us -> 34.7 us  [fused_device(): pl.pallas_call(functools.partial(kernel, n), out_shape=jax.ShapeDtypeStru...]
where the time goes in v5:
time: 36.4 us; the launch traced here: 36.2 us
  Pallas kernels  34.7 us (95%)
  local copies, waits for them, and re-layouts  1.47 us (4%)
    pallas_call x1, Pallas kernels, fused_device(): pl.pallas_call(functools.partial(kernel, n), out_shape=jax.ShapeDtypeStru...  34.7 us
    unnamed x3, local copies, waits for them, and re-layouts  1.47 us

profile of v5, /device:TPU:0, one launch (start us, length us, event | category | flops | bytes accessed | tf_op | source)
XLA Modules:
  0.0 36.2 jit_solution(16382666339893601237)
XLA Ops:
  0.0 0.0 copy-start
  0.0 0.7 %copy-done = s32[32]{0:T(128)S(1)} copy-done((s32[32]{0:T(128)S(1)}, s32[32]{0:T(128)}, u32[]{:S(2)}) %copy-start) | copy-done | bytes 152
  0.7 34.7 %shard_map.28 = f32[2,4,48,384]{3,2,1,0:T(8,128)S(1)} custom-call(s32[32]{0:T(128)S(1)} %copy-done, bf16[384,8192]{1,0:T(8,128)(2,1)} %rec_ref.1), custom_call_target="tpu_custom_call" | custom-call | tf_op jit(solution)/shard_map/pallas_call | solution.py:375
  35.4 0.8 %copy.4 = f32[2,4,384,48]{2,3,1,0:T(8,128)} copy(f32[2,4,384,48]{2,3,1,0:T(8,128)S(1)} %bitcast.1) | data formatting | bytes 1179648
Async XLA Ops:
  0.0 0.7 %copy-start = (s32[32]{0:T(128)S(1)}, s32[32]{0:T(128)}, u32[]{:S(2)}) copy-start(s32[32]{0:T(128)} %fire_hbm.1) | copy-start | bytes 388

commit v6 on v4

--- a/solution.py
+++ b/solution.py
@@ -235,8 +235,8 @@
             col_near(src, h).start()
 
     def send_own(h):
-        ring(me, h, 0).start()
-        ring(me, h, 1).start()
+        ring(me, h, h).start()
+        ring(me, h, 1 - h).start()
         share(me, h).start()
         send_col(me, h)
 

time: 35.1 us -> 35.1 us (level)
  no operation moved by 1% of the time
where the time goes in v6:
time: 35.1 us; the launch traced here: 34.4 us
  Pallas kernels  32.9 us (94%)
  local copies, waits for them, and re-layouts  1.47 us (4%)
    pallas_call x1, Pallas kernels, fused_device(): pl.pallas_call(functools.partial(kernel, n), out_shape=jax.ShapeDtypeStru...  32.9 us
    unnamed x3, local copies, waits for them, and re-layouts  1.47 us

profile of v6, /device:TPU:0, one launch (start us, length us, event | category | flops | bytes accessed | tf_op | source)
XLA Modules:
  0.0 34.4 jit_solution(11351892366168523700)
XLA Ops:
  0.0 0.0 copy-start
  0.0 0.7 %copy-done = s32[32]{0:T(128)S(1)} copy-done((s32[32]{0:T(128)S(1)}, s32[32]{0:T(128)}, u32[]{:S(2)}) %copy-start) | copy-done | bytes 152
  0.7 32.9 %shard_map.28 = f32[2,4,48,384]{3,2,1,0:T(8,128)S(1)} custom-call(s32[32]{0:T(128)S(1)} %copy-done, bf16[384,8192]{1,0:T(8,128)(2,1)} %rec_ref.1), custom_call_target="tpu_custom_call" | custom-call | tf_op jit(solution)/shard_map/pallas_call | solution.py:364
  33.6 0.8 %copy.4 = f32[2,4,384,48]{2,3,1,0:T(8,128)} copy(f32[2,4,384,48]{2,3,1,0:T(8,128)S(1)} %bitcast.1) | data formatting | bytes 1179648
Async XLA Ops:
  0.0 0.7 %copy-start = (s32[32]{0:T(128)S(1)}, s32[32]{0:T(128)}, u32[]{:S(2)}) copy-start(s32[32]{0:T(128)} %fire_hbm.1) | copy-start | bytes 388
